TPU v7x, 256 devices: a whole 4x4x8 slice. The times are simulated.
256 devices in a mesh: patch: 32 (over y, z), req: 4 (over x), owner: 2 (over core).
Axes of the slice: x: 4, y: 4, z: 8, core: 2. Of those that a mesh axis runs over, the one named last changes fastest.
Arguments:
- latents: bfloat16 [8, 256, 256, 320], P('req', 'patch', 'owner'), may hold values from -24 to 24
- timestep_embedding: bfloat16 [8, 1280], P('req'), may hold values from -6 to 6
- embedding_weight: bfloat16 [1280, 320], replicated, may hold values from -0.15625 to 0.15625
- group_norm_gain: float32 [2, 320], replicated, may hold values from 0.25 to 1.75
- group_norm_shift: float32 [2, 320], replicated, may hold values from -3 to 3
- kernel_weight: bfloat16 [2, 9, 320, 320], replicated, may hold values from -0.109375 to 0.109375
- plugin_reduce_library: bfloat16 [8, 2, 184320], P(('req', 'owner'), None, 'patch'), may hold values from -0.109375 to 0.109375
- plugin_expand_library: bfloat16 [8, 2, 20480], P(('req', 'owner'), None, 'patch'), may hold values from -0.75 to 0.75
- image_adapter: int32 [8, 1], P('req'), may hold values from 0 to 7
- adapter_bank_row: int32 [8], replicated, may hold values from 0 to 7, each once
Outputs:
- result: bfloat16 [8, 256, 256, 320], P('req', 'patch', 'owner')
Inputs may be any that keep to these rules, and one draw needn't show every extreme that they name: `image_adapter`: each image names one adapter; every adapter is named by some image. A permutation: adapter a is stored in bank row adapter_bank_row[a].
All inputs are finite; a program needn't handle non-finite values.
Results may differ from a plain program's by a relative error of at most 0.0055.
Values may be sent and summed in bfloat16 or wider, within the bound.
A program may use at most 128 MiB of HBM per device.

v0:
```python
import jax
import jax.numpy as jnp
from jax import lax
from jax.sharding import PartitionSpec as P

GROUPS = 32


def padded_2(block, sides, width):
    for axis, dim in sides:
        count = lax.axis_size(axis)
        forward = [(i, i + 1) for i in range(count - 1)]
        backward = [(target, source) for source, target in forward]
        low = lax.ppermute(
            lax.slice_in_dim(block, block.shape[dim] - width, None, axis=dim), axis, forward
        )
        high = lax.ppermute(lax.slice_in_dim(block, 0, width, axis=dim), axis, backward)
        block = jnp.concatenate([low, block, high], axis=dim)
    return block


def group_act(values, gain, shift):
    images, rows, columns, chans = values.shape
    grouped = values.reshape(images, rows, columns, GROUPS, chans // GROUPS)
    count = rows * columns * (chans // GROUPS) * lax.axis_size("patch") * lax.axis_size("owner")
    total = lax.psum(jnp.sum(grouped, axis=(1, 2, 4)), ("patch", "owner"))
    mean = total / count
    centered = grouped - mean[:, None, None, :, None]
    spread = lax.psum(jnp.sum(centered * centered, axis=(1, 2, 4)), ("patch", "owner"))
    var = spread / count
    normed = (centered / jnp.sqrt(var + 1e-05)[:, None, None, :, None]).reshape(values.shape)
    return jax.nn.silu(normed * gain + shift).astype(jnp.bfloat16)


def block_conv(act, kernel, reducing_filter, expanding_linear_map):
    images, rows, columns, chans = act.shape
    outward = kernel.shape[2]
    padded = padded_2(act, (("patch", 1), ("owner", 2)), 1)
    joined = jnp.concatenate(
        [jnp.broadcast_to(kernel[None], (images,) + kernel.shape), reducing_filter], axis=3
    )
    accum = jnp.zeros((images, rows, columns, joined.shape[3]), jnp.float32)
    for tap in range(9):
        row_off, col_off = divmod(tap, 3)
        window = padded[:, row_off : row_off + rows, col_off : col_off + columns, :]
        accum = accum + jnp.einsum(
            "bhwc,bcd->bhwd", window, joined[:, tap], preferred_element_type=jnp.float32
        )
    lowpart = accum[..., outward:].astype(jnp.bfloat16)
    return accum[..., :outward] + jnp.einsum(
        "bhwr,brd->bhwd", lowpart, expanding_linear_map, preferred_element_type=jnp.float32
    )


def local(
    latents,
    timestep_embedding,
    embedding_weight,
    group_norm_gain,
    group_norm_shift,
    kernel_weight,
    plugin_reduce_library,
    plugin_expand_library,
    image_adapter,
    adapter_bank_row,
):
    images, rows, columns, chans = latents.shape
    wanted = image_adapter[:, 0]
    table = jnp.arange(adapter_bank_row.shape[0], dtype=jnp.int32)
    slots = jnp.sum(
        jnp.where(wanted[:, None] == table[None, :], adapter_bank_row[None, :], 0), axis=1
    )
    full_down, full_up = (
        lax.all_gather(plugin_reduce_library, "patch", axis=2, tiled=True),
        lax.all_gather(plugin_expand_library, "patch", axis=2, tiled=True),
    )
    pieces = (
        lax.all_gather(full_down, ("req", "owner"), axis=0, tiled=True),
        lax.all_gather(full_up, ("req", "owner"), axis=0, tiled=True),
    )
    count = pieces[0].shape[0]
    match = (slots[:, None] == jnp.arange(count, dtype=jnp.int32)[None, :]).astype(jnp.bfloat16)
    first = jnp.einsum("ik,kjs->ijs", match, pieces[0], preferred_element_type=jnp.float32)
    second = jnp.einsum("ik,kjs->ijs", match, pieces[1], preferred_element_type=jnp.float32)
    down_sel = first.astype(jnp.bfloat16)
    up_sel = second.astype(jnp.bfloat16)
    rank = up_sel.shape[2] // chans
    down_all = down_sel.reshape(images, 2, 9, chans, rank)
    up_all = up_sel.reshape(images, 2, rank, chans)
    temb = jax.nn.silu(timestep_embedding.astype(jnp.float32)).astype(jnp.bfloat16)
    proj = jnp.dot(temb, embedding_weight, preferred_element_type=jnp.float32)
    source = latents.astype(jnp.float32)
    act1 = group_act(source, group_norm_gain[0], group_norm_shift[0])
    hidden1 = (
        block_conv(act1, kernel_weight[0], down_all[:, 0], up_all[:, 0]) + proj[:, None, None, :]
    ).astype(jnp.bfloat16)
    act2 = group_act(hidden1.astype(jnp.float32), group_norm_gain[1], group_norm_shift[1])
    result = source + block_conv(act2, kernel_weight[1], down_all[:, 1], up_all[:, 1])
    return result.astype(jnp.bfloat16)


def solution(mesh):
    in_specs = (
        P("req", "patch", "owner", None),
        P("req", None),
        P(),
        P(),
        P(),
        P(),
        P(("req", "owner"), None, "patch"),
        P(("req", "owner"), None, "patch"),
        P("req", None),
        P(),
    )
    out_specs = P("req", "patch", "owner", None)
    return jax.shard_map(local, mesh=mesh, in_specs=in_specs, out_specs=out_specs, check_vma=False)
```

profile of v0, /device:TPU:1, one launch (start us, length us, event | category | flops | bytes accessed | tf_op | source)
XLA Modules:
  0.0 778.4 jit_solution(10491722644223189108)
XLA Ops:
  6.6 47.2 %all_gather.12 = bf16[1,2,184320]{2,1,0:T(2,128)(2,1)} all-gather(bf16[1,2,5760]{2,1,0:T(2,128)(2,1)} %param.16), channel_id=1, replica_groups=mesh['patch'=32,'req'=4,'owner'=2] {'patch'}, dimensions={2}, use_global_device_ids=true | all-gather | bytes 760320 | tf_op jit(solution)/shard_map/all_gather | solution.py:74
  55.6 135.6 %psum.28 = f32[2,32]{1,0:T(2,128)S(1)} all-reduce(f32[2,32]{1,0:T(2,128)S(1)} %reduce_sum.59), channel_id=1, replica_groups=mesh['patch'=32,'req'=4,'owner'=2] {'patch','owner'}, use_global_device_ids=true, to_apply=%region_2.3 | all-reduce | flops 64 | bytes 512 | tf_op jit(solution)/shard_map/psum | solution.py:26
  192.2 124.0 %psum.29 = f32[2,32]{1,0:T(2,128)S(1)} all-reduce(f32[2,32]{1,0:T(2,128)S(1)} %reduce_sum.62), channel_id=1, replica_groups=mesh['patch'=32,'req'=4,'owner'=2] {'patch','owner'}, use_global_device_ids=true, to_apply=%region_5.6 | all-reduce | flops 64 | bytes 512 | tf_op jit(solution)/shard_map/psum | solution.py:29
  320.5 32.0 %all_gather.14 = bf16[1,2,20480]{2,1,0:T(2,128)(2,1)S(1)} all-gather(bf16[1,2,640]{2,1,0:T(2,128)(2,1)S(1)} %copy-done.16), channel_id=1, replica_groups=mesh['patch'=32,'req'=4,'owner'=2] {'patch'}, dimensions={2}, use_global_device_ids=true | all-gather | bytes 84480 | tf_op jit(solution)/shard_map/all_gather | solution.py:75
  352.5 24.4 %all_gather.15 = bf16[8,2,20480]{2,1,0:T(2,128)(2,1)S(1)} all-gather(bf16[1,2,20480]{2,1,0:T(2,128)(2,1)S(1)} %all_gather.14), channel_id=1, replica_groups=mesh['patch'=32,'req'=4,'owner'=2] {'req','owner'}, dimensions={0}, use_global_device_ids=true | all-gather | bytes 737280 | tf_op jit(solution)/shard_map/all_gather | solution.py:79
  377.0 4.8 slice_bitcast_fusion
  390.1 3.5 collective-permute-start.3
  398.0 5.7 pad_maximum_fusion
  403.7 10.7 %convolution_convert_fusion = bf16[2,2,184320]{2,0,1:T(2,128)(2,1)} fusion(bf16[8,2,184320]{2,1,0:T(2,128)(2,1)} %all-gather.2.cloned.1.call-done, s32[2]{0:T(128)S(1)} %fusion.123), kind=kOutput, calls=%fused_computation | convolution fusion | flops 12533776 | bytes 7372808 | tf_op jit(solution)/shard_map/ik,kjs->ijs/dot_general | solution.py:83
  414.4 4.7 reshape.54
  419.1 3.3 fusion.145
  425.4 2.7 fusion.52
  428.2 2.9 fusion.54
  431.1 2.9 fusion.50
  434.0 2.7 fusion.48
  436.7 2.7 fusion.80
  439.4 2.7 fusion.14
  442.2 2.7 fusion.18
  444.9 9.6 %add_add_fusion.1 = f32[2,8,128,384]{2,3,1,0:T(8,128)} fusion(f32[2,8,128,384]{2,3,1,0:T(8,128)} %fusion.18, f32[2,8,128,384]{2,3,1,0:T(8,128)} %fusion.48, f32[2,8,128,384]{2,3,1,0:T(8,128)} %fusion.50, f32[2,8,128,384]{2,3,1,0:T(8,128)} %fusion.80, f32[2,8,128,384]{2,3,1,0:T(8,128)S(1)} %copy-done.10, f32[2,8,128,384]{2,3,1,0:T(8,128)} %fusion.54, ...), kind=kOutput, calls=%fused_computation.45 | convolution fusion | flops 510590976 | bytes 35520512 | tf_op jit(solution)/shard_map/bhwc,bcd->bhwd/dot_general | solution.py:46
  457.3 122.8 %psum.30 = f32[2,32]{1,0:T(2,128)S(1)} all-reduce(f32[2,32]{1,0:T(2,128)S(1)} %reduce_sum.82), channel_id=1, replica_groups=mesh['patch'=32,'req'=4,'owner'=2] {'patch','owner'}, use_global_device_ids=true, to_apply=%region_9.10 | all-reduce | flops 64 | bytes 512 | tf_op jit(solution)/shard_map/psum | solution.py:26
  581.0 127.5 %psum.31 = f32[2,32]{1,0:T(2,128)S(1)} all-reduce(f32[2,32]{1,0:T(2,128)S(1)} %reduce_sum.85), channel_id=1, replica_groups=mesh['patch'=32,'req'=4,'owner'=2] {'patch','owner'}, use_global_device_ids=true, to_apply=%region_12.13 | all-reduce | flops 64 | bytes 512 | tf_op jit(solution)/shard_map/psum | solution.py:29
  714.9 3.2 fusion.97
  727.7 3.7 collective-permute-start.7
  731.4 4.1 fusion.22
  735.5 2.7 fusion.26
  741.8 5.0 pad_maximum_fusion.1
  746.8 2.7 fusion.42
  749.5 2.7 fusion.38
  752.2 2.9 fusion.40
  755.1 2.9 fusion.36
  758.0 2.7 fusion.34
  760.7 8.9 %add_add_fusion = f32[2,8,128,384]{2,3,1,0:T(8,128)S(1)} fusion(f32[2,8,128,384]{2,3,1,0:T(8,128)} %fusion.26, f32[2,8,128,384]{2,3,1,0:T(8,128)} %fusion.34, f32[2,8,128,384]{2,3,1,0:T(8,128)} %fusion.36, f32[2,8,128,384]{2,3,1,0:T(8,128)S(1)} %copy-done.9, f32[2,8,128,384]{2,3,1,0:T(8,128)} %fusion.38, f32[2,8,128,384]{2,3,1,0:T(8,128)} %fusion.40, ...), kind=kOutput, calls=%fused_computation.44 | convolution fusion | flops 510590976 | bytes 35520512 | tf_op jit(solution)/shard_map/bhwc,bcd->bhwd/dot_general | solution.py:46
  (116 shorter events, 47.3 us)
Async XLA Ops:
  6.5 375.3 %copy-start = (bf16[1280,320]{0,1:T(8,128)(2,1)S(1)}, bf16[1280,320]{0,1:T(8,128)(2,1)}, u32[]{:S(2)}) copy-start(bf16[1280,320]{0,1:T(8,128)(2,1)} %param.12) | copy-start | bytes 2457604
  6.5 184.9 %copy-start.5 = (bf16[2,8,128,320]{2,3,1,0:T(8,128)(2,1)S(1)}, bf16[2,8,128,320]{2,3,1,0:T(8,128)(2,1)}, u32[]{:S(2)}) copy-start(bf16[2,8,128,320]{2,3,1,0:T(8,128)(2,1)} %param.10) | copy-start | bytes 3932164
  6.5 309.9 %copy-start.15 = (f32[2,320]{1,0:T(2,128)S(1)}, f32[2,320]{1,0:T(2,128)}, u32[]{:S(2)}) copy-start(f32[2,320]{1,0:T(2,128)} %param.13) | copy-start | bytes 7684
  6.5 309.9 %copy-start.14 = (f32[2,320]{1,0:T(2,128)S(1)}, f32[2,320]{1,0:T(2,128)}, u32[]{:S(2)}) copy-start(f32[2,320]{1,0:T(2,128)} %param.14) | copy-start | bytes 7684
  6.5 397.2 %all-gather.2.cloned.1.call-start = ((), (), s32[]{:S(2)}) async-start(), calls=%async_computation | async-start | bytes 6635520 | tf_op jit(solution)/shard_map/all_gather | solution.py:78
  53.8 266.6 %copy-start.16 = (bf16[1,2,640]{2,1,0:T(2,128)(2,1)S(1)}, bf16[1,2,640]{2,1,0:T(2,128)(2,1)}, u32[]{:S(2)}) copy-start(bf16[1,2,640]{2,1,0:T(2,128)(2,1)} %param.17) | copy-start | bytes 7684
  317.9 64.4 %collective-permute-start = (bf16[2,1,128,320]{2,3,1,0:T(8,128)(2,1)S(1)}, bf16[2,1,128,320]{2,3,1,0:T(8,128)(2,1)S(1)}, u32[]{:S(2)}, u32[]{:S(2)}) collective-permute-start(bf16[2,1,128,320]{2,3,1,0:T(8,128)(2,1)S(1)} %get-tuple-element.23), channel_id=1, source_target_pairs={{0,8},{8,16},{16,24},{24,32},{32,40},{40,48},{48,56},{56,64},{64,7... | collective-permute-start | bytes 491528 | tf_op jit(solution)/shard_map/ppermute | solution.py:14
  319.2 63.1 %collective-permute-start.1 = (bf16[2,1,128,320]{2,3,1,0:T(8,128)(2,1)S(1)}, bf16[2,1,128,320]{2,3,1,0:T(8,128)(2,1)S(1)}, u32[]{:S(2)}, u32[]{:S(2)}) collective-permute-start(bf16[2,1,128,320]{2,3,1,0:T(8,128)(2,1)S(1)} %get-tuple-element.24), channel_id=1, source_target_pairs={{8,0},{16,8},{24,16},{32,24},{40,32},{48,40},{56,48},{64,56},{72,6... | collective-permute-start | bytes 491528 | tf_op jit(solution)/shard_map/ppermute | solution.py:17
  377.0 4.8 copy-start.13
  377.0 5.1 copy-start.17
  377.0 5.1 copy-start.18
  386.9 7.8 collective-permute-start.2
  390.1 6.3 collective-permute-start.3
  419.1 3.4 copy-start.12
  422.5 1.9 copy-start.8
  425.4 2.7 copy-start.7
  442.2 2.7 copy-start.10
  708.7 5.5 copy-start.11
  710.1 9.8 %copy-start.3 = (bf16[2,8,128,320]{2,3,1,0:T(8,128)(2,1)}, bf16[2,8,128,320]{2,3,1,0:T(8,128)(2,1)S(1)}, u32[]{:S(2)}) copy-start(bf16[2,8,128,320]{2,3,1,0:T(8,128)(2,1)S(1)} %multiply_convert_fusion) | copy-start | bytes 3932164
  710.2 7.9 %collective-permute-start.4 = (bf16[2,1,128,320]{2,3,1,0:T(8,128)(2,1)S(1)}, bf16[2,1,128,320]{2,3,1,0:T(8,128)(2,1)S(1)}, u32[]{:S(2)}, u32[]{:S(2)}) collective-permute-start(bf16[2,1,128,320]{2,3,1,0:T(8,128)(2,1)S(1)} %get-tuple-element.21), channel_id=1, source_target_pairs={{0,8},{8,16},{16,24},{24,32},{32,40},{40,48},{48,56},{56,64},{64,7... | collective-permute-start | bytes 491528 | tf_op jit(solution)/shard_map/ppermute | solution.py:14
  712.9 7.0 collective-permute-start.5
  714.8 3.2 copy-start.2
  724.4 13.8 %collective-permute-start.6 = (bf16[2,10,1,320]{3,0,2,1:T(2,128)(2,1)S(1)}, bf16[2,10,1,320]{3,0,2,1:T(2,128)(2,1)S(1)}, u32[]{:S(2)}, u32[]{:S(2)}) collective-permute-start(bf16[2,10,1,320]{3,0,2,1:T(2,128)(2,1)S(1)} %copy.104), channel_id=1, source_target_pairs={{0,1},{2,3},{4,5},{6,7},{8,9},{10,11},{12,13},{14,15},{16,17},{18,... | collective-permute-start | bytes 38408 | tf_op jit(solution)/shard_map/ppermute | solution.py:14
  725.7 9.8 %slice-start = ((s8[4423680]{0:T(1024)(128)(4,1)}), s8[229376]{0:T(1024)(128)(4,1)S(1)}, s32[]{:S(2)}) async-start(s8[4423680]{0:T(1024)(128)(4,1)} %bitcast.145), calls=%async_computation.1 | async-start | bytes 458752
  727.7 7.8 %slice-start.1 = ((s8[4423680]{0:T(1024)(128)(4,1)}), s8[4194304]{0:T(1024)(128)(4,1)S(1)}, s32[]{:S(2)}) async-start(s8[4423680]{0:T(1024)(128)(4,1)} %bitcast.145), calls=%async_computation.2 | async-start | bytes 8388608
  727.7 7.8 %copy-start.4 = (bf16[2,8,128,320]{2,3,1,0:T(8,128)(2,1)S(1)}, bf16[2,8,128,320]{2,3,1,0:T(8,128)(2,1)}, u32[]{:S(2)}) copy-start(bf16[2,8,128,320]{2,3,1,0:T(8,128)(2,1)} %copy-done.3) | copy-start | bytes 3932164
  727.7 12.5 %collective-permute-start.7 = (bf16[2,10,1,320]{3,0,2,1:T(2,128)(2,1)S(1)}, bf16[2,10,1,320]{3,0,2,1:T(2,128)(2,1)S(1)}, u32[]{:S(2)}, u32[]{:S(2)}) collective-permute-start(bf16[2,10,1,320]{3,0,2,1:T(2,128)(2,1)S(1)} %copy.109), channel_id=1, source_target_pairs={{1,0},{3,2},{5,4},{7,6},{9,8},{11,10},{13,12},{15,14},{17,16},{19,... | collective-permute-start | bytes 38408 | tf_op jit(solution)/shard_map/ppermute | solution.py:17
  740.1 6.7 slice-start.2
  741.8 5.0 slice-start.3
  758.0 2.7 copy-start.9
  760.7 8.9 %copy-start.6 = (bf16[2,8,128,320]{2,3,1,0:T(8,128)(2,1)S(1)}, bf16[2,8,128,320]{2,3,1,0:T(8,128)(2,1)}, u32[]{:S(2)}) copy-start(bf16[2,8,128,320]{2,3,1,0:T(8,128)(2,1)} %param.10) | copy-start | bytes 3932164
  760.7 10.6 %copy-start.1 = (bf16[1280,320]{0,1:T(8,128)(2,1)S(1)}, bf16[1280,320]{0,1:T(8,128)(2,1)}, u32[]{:S(2)}) copy-start(bf16[1280,320]{0,1:T(8,128)(2,1)} %param.12) | copy-start | bytes 2457604
Sparse Core Ops, SparseCore 0:
  54.0 51.1 all-gather.1
where the time goes:
time: 784 us; the launch traced here: 778 us
  blocking collectives  614 us (78%)
  matrix products  79 us (10%)
  local copies, waits for them, and re-layouts  37.7 us (5%)
  other arithmetic  17 us (2%)
  starting transfers between devices  15 us (2%)
  between operations  14.1 us (2%)
    psum x2, blocking collectives, group_act(): total = lax.psum(jnp.sum(grouped, axis=(1, 2, 4)), ('patch', 'owner'))  258 us
    psum x2, blocking collectives, group_act(): lax.psum(jnp.sum(centered * centered, axis=(1, 2, 4)), ('patch', 'owner'))  252 us
    dot_general x18, matrix products, block_conv(): jnp.einsum('bhwc,bcd->bhwd', window, joined[:, tap], preferred_element_ty...  62.9 us
    all_gather x1, blocking collectives, local(): lax.all_gather(plugin_reduce_library, 'patch', axis=2, tiled=True)  47.2 us
    all_gather x1, blocking collectives, local(): lax.all_gather(plugin_expand_library, 'patch', axis=2, tiled=True)  32 us
    all_gather x1, blocking collectives, local(): lax.all_gather(full_up, ('req', 'owner'), axis=0, tiled=True)  24.4 us
  transfers between devices with their start and end apart: 9, of which 1 were waited for; matrix products, arithmetic and copies ran while one was open for 5% of the time, Pallas kernels for 0%

commit v1 on v0

--- a/solution.py
+++ b/solution.py
@@ -4,6 +4,28 @@
 from jax.sharding import PartitionSpec as P
 
 GROUPS = 32
+
+
+def laid_out(pieces, dim):
+    lengths = list(pieces.shape[1:])
+    lengths[dim] *= pieces.shape[0]
+    return jnp.moveaxis(pieces, 0, dim).reshape(lengths)
+
+
+def gather_around(value, axis, dim):
+    count = lax.axis_size(axis)
+    pairs = [(i, (i + 1) % count) for i in range(count)]
+    back = [(b, a) for a, b in pairs]
+    lower, upper = ([], [])
+    for turn in range(count - 1):
+        if turn % 2 == 0:
+            lower.append(lax.ppermute(lower[-1] if lower else value, axis, pairs))
+        else:
+            upper.append(lax.ppermute(upper[-1] if upper else value, axis, back))
+    blocks = jnp.stack([*lower[::-1], value, *upper])
+    shift = lax.axis_index(axis) - len(lower)
+    blocks = blocks[(jnp.arange(count) - shift) % count]
+    return laid_out(blocks, dim)
 
 
 def padded_2(block, sides, width):
@@ -76,7 +98,7 @@
     )
     pieces = (
         lax.all_gather(full_down, ("req", "owner"), axis=0, tiled=True),
-        lax.all_gather(full_up, ("req", "owner"), axis=0, tiled=True),
+        gather_around(full_up, ("req", "owner"), 0),
     )
     count = pieces[0].shape[0]
     match = (slots[:, None] == jnp.arange(count, dtype=jnp.int32)[None, :]).astype(jnp.bfloat16)

time: 784 us -> 793 us (1.011)
  blocking collectives: 614 us -> 582 us
  starting transfers between devices: 15 us -> 43 us
    ppermute x0 -> x7, starting transfers between devices: none -> 27.9 us  [the longest x4 27.4 us: gather_around(): lower.append(lax.ppermute(lower[-1] if lower else value, axis, pairs))]
    all_gather x1 -> x0, blocking collectives: 24.4 us -> none  [local(): lax.all_gather(full_up, ('req', 'owner'), axis=0, tiled=True)]
    psum x2, blocking collectives: 258 us -> 249 us  [group_act(): total = lax.psum(jnp.sum(grouped, axis=(1, 2, 4)), ('patch', 'owner'))]
  transfers between devices with their start and end apart: 9 -> 16, of which waited for: 1 -> 2; matrix products, arithmetic and copies ran while one was open for 5% -> 6% of each run, Pallas kernels for 0% -> 0%
where the time goes in v1:
time: 793 us; the launch traced here: 787 us
  blocking collectives  582 us (73%)
  matrix products  78.8 us (10%)
  local copies, waits for them, and re-layouts  43.3 us (5%)
  starting transfers between devices  43 us (5%)
  other arithmetic  18.8 us (2%)
  between operations  14.2 us (2%)
    psum x2, blocking collectives, group_act(): lax.psum(jnp.sum(centered * centered, axis=(1, 2, 4)), ('patch', 'owner'))  254 us
    psum x2, blocking collectives, group_act(): total = lax.psum(jnp.sum(grouped, axis=(1, 2, 4)), ('patch', 'owner'))  249 us
    dot_general x18, matrix products, block_conv(): jnp.einsum('bhwc,bcd->bhwd', window, joined[:, tap], preferred_element_ty...  62.7 us
    all_gather x1, blocking collectives, local(): lax.all_gather(plugin_reduce_library, 'patch', axis=2, tiled=True)  41.6 us
    all_gather x1, blocking collectives, local(): lax.all_gather(plugin_expand_library, 'patch', axis=2, tiled=True)  37.3 us
    ppermute x4, starting transfers between devices, gather_around(): lower.append(lax.ppermute(lower[-1] if lower else value, axis, pairs))  27.4 us
  transfers between devices with their start and end apart: 16, of which 2 were waited for; matrix products, arithmetic and copies ran while one was open for 6% of the time, Pallas kernels for 0%

profile of v1, /device:TPU:1, one launch (start us, length us, event | category | flops | bytes accessed | tf_op | source)
XLA Modules:
  0.0 786.6 jit_solution(9320526253211742672)
XLA Ops:
  6.5 37.3 %all_gather.11 = bf16[1,2,20480]{2,1,0:T(2,128)(2,1)S(1)} all-gather(bf16[1,2,640]{2,1,0:T(2,128)(2,1)} %param.17), channel_id=1, replica_groups=mesh['patch'=32,'req'=4,'owner'=2] {'patch'}, dimensions={2}, use_global_device_ids=true | all-gather | bytes 84480 | tf_op jit(solution)/shard_map/all_gather | solution.py:97
  43.8 11.9 %collective-permute-start.4 = (bf16[1,2,20480]{2,1,0:T(2,128)(2,1)S(1)}, bf16[1,2,20480]{2,1,0:T(2,128)(2,1)}, u32[]{:S(2)}, u32[]{:S(2)}) collective-permute-start(bf16[1,2,20480]{2,1,0:T(2,128)(2,1)S(1)} %all_gather.11), channel_id=1, source_target_pairs={{0,1},{1,2},{2,3},{3,4},{4,5},{5,6},{6,7},{7,0},{8,9},{9,10},{10,1... | collective-permute-start | bytes 245768 | tf_op jit(solution)/shard_map/ppermute | solution.py:22
  57.5 125.3 %psum.28 = f32[2,32]{1,0:T(2,128)S(1)} all-reduce(f32[2,32]{1,0:T(2,128)S(1)} %reduce_sum.59), channel_id=1, replica_groups=mesh['patch'=32,'req'=4,'owner'=2] {'patch','owner'}, use_global_device_ids=true, to_apply=%region_2.3 | all-reduce | flops 64 | bytes 512 | tf_op jit(solution)/shard_map/psum | solution.py:48
  184.9 124.8 %psum.29 = f32[2,32]{1,0:T(2,128)S(1)} all-reduce(f32[2,32]{1,0:T(2,128)S(1)} %reduce_sum.62), channel_id=1, replica_groups=mesh['patch'=32,'req'=4,'owner'=2] {'patch','owner'}, use_global_device_ids=true, to_apply=%region_5.6 | all-reduce | flops 64 | bytes 512 | tf_op jit(solution)/shard_map/psum | solution.py:51
  315.3 41.6 %all_gather.9 = bf16[1,2,184320]{2,1,0:T(2,128)(2,1)} all-gather(bf16[1,2,5760]{2,1,0:T(2,128)(2,1)S(1)} %copy-done.13), channel_id=1, replica_groups=mesh['patch'=32,'req'=4,'owner'=2] {'patch'}, dimensions={2}, use_global_device_ids=true | all-gather | bytes 760320 | tf_op jit(solution)/shard_map/all_gather | solution.py:96
  357.0 4.8 slice_bitcast_fusion
  362.4 13.8 %collective-permute-start.5 = (bf16[1,2,20480]{2,1,0:T(2,128)(2,1)}, bf16[1,2,20480]{2,1,0:T(2,128)(2,1)S(1)}, u32[]{:S(2)}, u32[]{:S(2)}) collective-permute-start(bf16[1,2,20480]{2,1,0:T(2,128)(2,1)} %collective-permute-done.4), channel_id=1, source_target_pairs={{0,1},{1,2},{2,3},{3,4},{4,5},{5,6},{6,7},{7,0},{8,9},{9,10},{10,1... | collective-permute-start | bytes 245768 | tf_op jit(solution)/shard_map/ppermute | solution.py:22
  384.0 3.7 collective-permute-start.3
  393.3 6.2 pad_maximum_fusion
  404.8 4.2 all-gather.2.cloned.1.call-done
  409.1 10.7 %convolution_convert_fusion = bf16[2,2,184320]{2,0,1:T(2,128)(2,1)} fusion(bf16[8,2,184320]{2,1,0:T(2,128)(2,1)} %all-gather.2.cloned.1.call-done, s32[2]{0:T(128)S(1)} %fusion.123), kind=kOutput, calls=%fused_computation.1 | convolution fusion | flops 12533776 | bytes 7372808 | tf_op jit(solution)/shard_map/ik,kjs->ijs/dot_general | solution.py:105
  419.8 4.7 reshape.118
  424.5 3.3 fusion.147
  430.8 2.7 fusion.52
  433.6 2.9 fusion.54
  436.5 2.9 fusion.50
  439.4 2.7 fusion.48
  444.8 2.7 fusion.14
  447.5 2.7 fusion.18
  450.2 9.6 %add_add_fusion.1 = f32[2,8,128,384]{2,3,1,0:T(8,128)} fusion(f32[2,8,128,384]{2,3,1,0:T(8,128)} %fusion.18, f32[2,8,128,384]{2,3,1,0:T(8,128)} %fusion.48, f32[2,8,128,384]{2,3,1,0:T(8,128)} %fusion.50, f32[2,8,128,384]{2,3,1,0:T(8,128)} %fusion.80, f32[2,8,128,384]{2,3,1,0:T(8,128)S(1)} %copy-done.10, f32[2,8,128,384]{2,3,1,0:T(8,128)} %fusion.54, ...), kind=kOutput, calls=%fused_computation.46 | convolution fusion | flops 510590976 | bytes 35520512 | tf_op jit(solution)/shard_map/bhwc,bcd->bhwd/dot_general | solution.py:68
  462.7 124.2 %psum.30 = f32[2,32]{1,0:T(2,128)S(1)} all-reduce(f32[2,32]{1,0:T(2,128)S(1)} %reduce_sum.82), channel_id=1, replica_groups=mesh['patch'=32,'req'=4,'owner'=2] {'patch','owner'}, use_global_device_ids=true, to_apply=%region_9.10 | all-reduce | flops 64 | bytes 512 | tf_op jit(solution)/shard_map/psum | solution.py:48
  587.8 129.0 %psum.31 = f32[2,32]{1,0:T(2,128)S(1)} all-reduce(f32[2,32]{1,0:T(2,128)S(1)} %reduce_sum.85), channel_id=1, replica_groups=mesh['patch'=32,'req'=4,'owner'=2] {'patch','owner'}, use_global_device_ids=true, to_apply=%region_12.13 | all-reduce | flops 64 | bytes 512 | tf_op jit(solution)/shard_map/psum | solution.py:51
  723.2 3.2 fusion.97
  736.0 3.7 collective-permute-start.14
  739.7 4.1 fusion.22
  743.8 2.7 fusion.26
  750.1 5.0 pad_maximum_fusion.1
  755.1 2.7 fusion.42
  757.8 2.7 fusion.38
  760.5 2.9 fusion.40
  763.4 2.9 fusion.36
  768.9 8.9 %add_add_fusion = f32[2,8,128,384]{2,3,1,0:T(8,128)S(1)} fusion(f32[2,8,128,384]{2,3,1,0:T(8,128)} %fusion.26, f32[2,8,128,384]{2,3,1,0:T(8,128)} %fusion.34, f32[2,8,128,384]{2,3,1,0:T(8,128)} %fusion.36, f32[2,8,128,384]{2,3,1,0:T(8,128)S(1)} %copy-done.9, f32[2,8,128,384]{2,3,1,0:T(8,128)} %fusion.38, f32[2,8,128,384]{2,3,1,0:T(8,128)} %fusion.40, ...), kind=kOutput, calls=%fused_computation.45 | convolution fusion | flops 510590976 | bytes 35520512 | tf_op jit(solution)/shard_map/bhwc,bcd->bhwd/dot_general | solution.py:68
  (140 shorter events, 61.9 us)
Async XLA Ops:
  6.5 355.3 %copy-start = (bf16[1280,320]{0,1:T(8,128)(2,1)S(1)}, bf16[1280,320]{0,1:T(8,128)(2,1)}, u32[]{:S(2)}) copy-start(bf16[1280,320]{0,1:T(8,128)(2,1)} %param.12) | copy-start | bytes 2457604
  6.5 304.8 %copy-start.5 = (bf16[2,8,128,320]{2,3,1,0:T(8,128)(2,1)S(1)}, bf16[2,8,128,320]{2,3,1,0:T(8,128)(2,1)}, u32[]{:S(2)}) copy-start(bf16[2,8,128,320]{2,3,1,0:T(8,128)(2,1)} %param.10) | copy-start | bytes 3932164
  6.5 308.8 %copy-start.13 = (bf16[1,2,5760]{2,1,0:T(2,128)(2,1)S(1)}, bf16[1,2,5760]{2,1,0:T(2,128)(2,1)}, u32[]{:S(2)}) copy-start(bf16[1,2,5760]{2,1,0:T(2,128)(2,1)} %param.16) | copy-start | bytes 69124
  6.5 402.5 %all-gather.2.cloned.1.call-start = ((), (), s32[]{:S(2)}) async-start(), calls=%async_computation | async-start | bytes 6635520 | tf_op jit(solution)/shard_map/all_gather | solution.py:100
  43.8 318.5 %collective-permute-start.4 = (bf16[1,2,20480]{2,1,0:T(2,128)(2,1)S(1)}, bf16[1,2,20480]{2,1,0:T(2,128)(2,1)}, u32[]{:S(2)}, u32[]{:S(2)}) collective-permute-start(bf16[1,2,20480]{2,1,0:T(2,128)(2,1)S(1)} %all_gather.11), channel_id=1, source_target_pairs={{0,1},{1,2},{2,3},{3,4},{4,5},{5,6},{6,7},{7,0},{8,9},{9,10},{10,1... | collective-permute-start | bytes 245768 | tf_op jit(solution)/shard_map/ppermute | solution.py:22
  55.7 320.4 %collective-permute-start.8 = (bf16[1,2,20480]{2,1,0:T(2,128)(2,1)S(1)}, bf16[1,2,20480]{2,1,0:T(2,128)(2,1)}, u32[]{:S(2)}, u32[]{:S(2)}) collective-permute-start(bf16[1,2,20480]{2,1,0:T(2,128)(2,1)S(1)} %all_gather.11), channel_id=1, source_target_pairs={{1,0},{2,1},{3,2},{4,3},{5,4},{6,5},{7,6},{0,7},{9,8},{10,9},{11,1... | collective-permute-start | bytes 245768 | tf_op jit(solution)/shard_map/ppermute | solution.py:24
  312.7 63.4 %collective-permute-start = (bf16[2,1,128,320]{2,3,1,0:T(8,128)(2,1)S(1)}, bf16[2,1,128,320]{2,3,1,0:T(8,128)(2,1)S(1)}, u32[]{:S(2)}, u32[]{:S(2)}) collective-permute-start(bf16[2,1,128,320]{2,3,1,0:T(8,128)(2,1)S(1)} %get-tuple-element.23), channel_id=1, source_target_pairs={{0,8},{8,16},{16,24},{24,32},{32,40},{40,48},{48,56},{56,64},{64,7... | collective-permute-start | bytes 491528 | tf_op jit(solution)/shard_map/ppermute | solution.py:36
  314.0 62.1 %collective-permute-start.1 = (bf16[2,1,128,320]{2,3,1,0:T(8,128)(2,1)S(1)}, bf16[2,1,128,320]{2,3,1,0:T(8,128)(2,1)S(1)}, u32[]{:S(2)}, u32[]{:S(2)}) collective-permute-start(bf16[2,1,128,320]{2,3,1,0:T(8,128)(2,1)S(1)} %get-tuple-element.24), channel_id=1, source_target_pairs={{8,0},{16,8},{24,16},{32,24},{40,32},{48,40},{56,48},{64,56},{72,6... | collective-permute-start | bytes 491528 | tf_op jit(solution)/shard_map/ppermute | solution.py:39
  357.0 5.1 copy-start.17
  357.0 5.1 copy-start.18
  362.4 25.3 %collective-permute-start.5 = (bf16[1,2,20480]{2,1,0:T(2,128)(2,1)}, bf16[1,2,20480]{2,1,0:T(2,128)(2,1)S(1)}, u32[]{:S(2)}, u32[]{:S(2)}) collective-permute-start(bf16[1,2,20480]{2,1,0:T(2,128)(2,1)} %collective-permute-done.4), channel_id=1, source_target_pairs={{0,1},{1,2},{2,3},{3,4},{4,5},{5,6},{6,7},{7,0},{8,9},{9,10},{10,1... | collective-permute-start | bytes 245768 | tf_op jit(solution)/shard_map/ppermute | solution.py:22
  376.1 11.6 %collective-permute-start.9 = (bf16[1,2,20480]{2,1,0:T(2,128)(2,1)}, bf16[1,2,20480]{2,1,0:T(2,128)(2,1)S(1)}, u32[]{:S(2)}, u32[]{:S(2)}) collective-permute-start(bf16[1,2,20480]{2,1,0:T(2,128)(2,1)} %collective-permute-done.8), channel_id=1, source_target_pairs={{1,0},{2,1},{3,2},{4,3},{5,4},{6,5},{7,6},{0,7},{9,8},{10,9},{11,1... | collective-permute-start | bytes 245768 | tf_op jit(solution)/shard_map/ppermute | solution.py:24
  380.8 7.4 collective-permute-start.2
  384.0 5.9 collective-permute-start.3
  387.7 3.9 collective-permute-start.6
  387.7 14.1 %collective-permute-start.10 = (bf16[1,2,20480]{2,1,0:T(2,128)(2,1)S(1)}, bf16[1,2,20480]{2,1,0:T(2,128)(2,1)S(1)}, u32[]{:S(2)}, u32[]{:S(2)}) collective-permute-start(bf16[1,2,20480]{2,1,0:T(2,128)(2,1)S(1)} %collective-permute-done.9), channel_id=1, source_target_pairs={{1,0},{2,1},{3,2},{4,3},{5,4},{6,5},{7,6},{0,7},{9,8},{10,9},{11,1... | collective-permute-start | bytes 245768 | tf_op jit(solution)/shard_map/ppermute | solution.py:24
  391.5 8.0 %collective-permute-start.7 = (bf16[1,2,20480]{2,1,0:T(2,128)(2,1)S(1)}, bf16[1,2,20480]{2,1,0:T(2,128)(2,1)S(1)}, u32[]{:S(2)}, u32[]{:S(2)}) collective-permute-start(bf16[1,2,20480]{2,1,0:T(2,128)(2,1)S(1)} %collective-permute-done.6), channel_id=1, source_target_pairs={{0,1},{1,2},{2,3},{3,4},{4,5},{5,6},{6,7},{7,0},{8,9},{9,10},{10,1... | collective-permute-start | bytes 245768 | tf_op jit(solution)/shard_map/ppermute | solution.py:22
  459.9 257.2 %copy-start.14 = (f32[320]{0:T(512)S(1)}, f32[320]{0:T(512)}, u32[]{:S(2)}) copy-start(f32[320]{0:T(512)} %get-tuple-element.7) | copy-start | bytes 3844
  459.9 257.2 %copy-start.15 = (f32[320]{0:T(512)S(1)}, f32[320]{0:T(512)}, u32[]{:S(2)}) copy-start(f32[320]{0:T(512)} %get-tuple-element.28) | copy-start | bytes 3844
  717.1 5.5 copy-start.11
  718.5 9.8 %copy-start.3 = (bf16[2,8,128,320]{2,3,1,0:T(8,128)(2,1)}, bf16[2,8,128,320]{2,3,1,0:T(8,128)(2,1)S(1)}, u32[]{:S(2)}) copy-start(bf16[2,8,128,320]{2,3,1,0:T(8,128)(2,1)S(1)} %multiply_convert_fusion) | copy-start | bytes 3932164
  718.5 7.9 %collective-permute-start.11 = (bf16[2,1,128,320]{2,3,1,0:T(8,128)(2,1)S(1)}, bf16[2,1,128,320]{2,3,1,0:T(8,128)(2,1)S(1)}, u32[]{:S(2)}, u32[]{:S(2)}) collective-permute-start(bf16[2,1,128,320]{2,3,1,0:T(8,128)(2,1)S(1)} %get-tuple-element.21), channel_id=1, source_target_pairs={{0,8},{8,16},{16,24},{24,32},{32,40},{40,48},{48,56},{56,64},{64,7... | collective-permute-start | bytes 491528 | tf_op jit(solution)/shard_map/ppermute | solution.py:36
  721.3 7.0 collective-permute-start.12
  732.7 13.8 %collective-permute-start.13 = (bf16[2,10,1,320]{3,0,2,1:T(2,128)(2,1)S(1)}, bf16[2,10,1,320]{3,0,2,1:T(2,128)(2,1)S(1)}, u32[]{:S(2)}, u32[]{:S(2)}) collective-permute-start(bf16[2,10,1,320]{3,0,2,1:T(2,128)(2,1)S(1)} %copy.104), channel_id=1, source_target_pairs={{0,1},{2,3},{4,5},{6,7},{8,9},{10,11},{12,13},{14,15},{16,17},{18,... | collective-permute-start | bytes 38408 | tf_op jit(solution)/shard_map/ppermute | solution.py:36
  734.0 9.8 %slice-start = ((s8[4423680]{0:T(1024)(128)(4,1)}), s8[229376]{0:T(1024)(128)(4,1)S(1)}, s32[]{:S(2)}) async-start(s8[4423680]{0:T(1024)(128)(4,1)} %bitcast.164), calls=%async_computation.1 | async-start | bytes 458752
  736.0 7.8 slice-start.1
  736.0 7.8 copy-start.4
  736.0 12.4 %collective-permute-start.14 = (bf16[2,10,1,320]{3,0,2,1:T(2,128)(2,1)S(1)}, bf16[2,10,1,320]{3,0,2,1:T(2,128)(2,1)S(1)}, u32[]{:S(2)}, u32[]{:S(2)}) collective-permute-start(bf16[2,10,1,320]{3,0,2,1:T(2,128)(2,1)S(1)} %copy.109), channel_id=1, source_target_pairs={{1,0},{3,2},{5,4},{7,6},{9,8},{11,10},{13,12},{15,14},{17,16},{19,... | collective-permute-start | bytes 38408 | tf_op jit(solution)/shard_map/ppermute | solution.py:39
  748.4 6.7 slice-start.2
  750.1 5.0 slice-start.3
  768.9 8.9 %copy-start.6 = (bf16[2,8,128,320]{2,3,1,0:T(8,128)(2,1)S(1)}, bf16[2,8,128,320]{2,3,1,0:T(8,128)(2,1)}, u32[]{:S(2)}) copy-start(bf16[2,8,128,320]{2,3,1,0:T(8,128)(2,1)} %param.10) | copy-start | bytes 3932164
  768.9 10.6 %copy-start.1 = (bf16[1280,320]{0,1:T(8,128)(2,1)S(1)}, bf16[1280,320]{0,1:T(8,128)(2,1)}, u32[]{:S(2)}) copy-start(bf16[1280,320]{0,1:T(8,128)(2,1)} %param.12) | copy-start | bytes 2457604
  (7 other events, 21.5 us)
Sparse Core Ops, SparseCore 0:
  357.1 51.9 all-gather.1
